TPU v7x, 32 devices: a whole 2x2x4 slice. The times are simulated.
32 devices in a mesh: slab: 8 (over z, y), band: 4 (over x, core).
Axes of the slice: x: 2, y: 2, z: 4, core: 2. Of those that a mesh axis runs over, the one named last changes fastest.
Arguments:
- orbitals: float32 [8, 128, 128, 128], P('band', 'slab'), may hold values from -6 to 6
Outputs:
- exchange_out: float32 [8, 128, 128, 128], P('band', 'slab')
All inputs are finite; a program needn't handle non-finite values.
Results may differ from a plain program's by a relative error of at most 0.00013.
Values sent between devices are 32-bit elements; how exact they have to be, the bound alone decides.
No kernel may reach another device: no remote copies, remote signals or barrier semaphores. Data moves between devices by JAX's collectives and lax.ppermute only.
A program may use at most 64 MiB of HBM per device.

v0:
```python
import math
import jax
import jax.numpy as jnp
from jax import lax
from jax.sharding import PartitionSpec as P

screen_width = 0.5
highest = lax.Precision.HIGHEST


def shifted(value, axis, steps):
    count = lax.axis_size(axis)
    pairs = [(source, (source + steps) % count) for source in range(count)]
    return lax.ppermute(value, axis, pairs)


def dft_tables(length):
    counter = jnp.arange(length, dtype=jnp.int32)
    product = counter[:, None] * counter[None, :] % length
    angles = 2.0 * math.pi / length * product.astype(jnp.float32)
    return (jnp.cos(angles), jnp.sin(angles))


def frequency(counter, length):
    return jnp.where(counter < length // 2, counter, counter - length).astype(jnp.float32)


def screened(squared):
    safe_sq = jnp.where(squared > 0, squared, 1.0)
    value = 4.0 * math.pi / safe_sq * (1.0 - jnp.exp(-safe_sq / (4.0 * screen_width**2)))
    return jnp.where(squared > 0, value, math.pi / screen_width**2)


def rotate(real_part, imag_part, cosine, sine_table, form, forward):
    sign = 1.0 if forward else -1.0
    real_cos = jnp.einsum(form, real_part, cosine, precision=highest)
    imag_sin = jnp.einsum(form, imag_part, sine_table, precision=highest)
    imag_cos = jnp.einsum(form, imag_part, cosine, precision=highest)
    real_sin = jnp.einsum(form, real_part, sine_table, precision=highest)
    return (real_cos + sign * imag_sin, imag_cos - sign * real_sin)


def potentials(density):
    count, planes, rows, columns = density.shape
    depth = planes * lax.axis_size("slab")
    cos_x, sin_x = dft_tables(columns)
    cos_y, sin_y = dft_tables(rows)
    cos_z, sin_z = dft_tables(depth)
    form_x = "pzyx,xk->pzyk"
    first = density[0::2]
    second = density[1::2]
    real_part = jnp.einsum(form_x, first, cos_x, precision=highest) + jnp.einsum(
        form_x, second, sin_x, precision=highest
    )
    imag_part = jnp.einsum(form_x, second, cos_x, precision=highest) - jnp.einsum(
        form_x, first, sin_x, precision=highest
    )
    real_part, imag_part = rotate(real_part, imag_part, cos_y, sin_y, "pzyx,yk->pzkx", True)
    part_re = lax.all_to_all(real_part, "slab", split_axis=2, concat_axis=1, tiled=True)
    part_im = lax.all_to_all(imag_part, "slab", split_axis=2, concat_axis=1, tiled=True)
    band_rows = part_re.shape[2]
    row_index = lax.axis_index("slab") * band_rows + jnp.arange(band_rows, dtype=jnp.int32)
    freq_z = frequency(jnp.arange(depth, dtype=jnp.int32), depth)
    freq_y = frequency(row_index, rows)
    freq_x = frequency(jnp.arange(columns, dtype=jnp.int32), columns)
    squared = ((2.0 * math.pi / depth * freq_z) ** 2)[:, None, None]
    squared = squared + ((2.0 * math.pi / rows * freq_y) ** 2)[None, :, None]
    squared = squared + ((2.0 * math.pi / columns * freq_x) ** 2)[None, None, :]
    weight = screened(squared)
    part_re, part_im = rotate(part_re, part_im, cos_z, sin_z, "pzyx,zk->pkyx", True)
    part_re = part_re * weight
    part_im = part_im * weight
    part_re, part_im = rotate(part_re, part_im, cos_z, sin_z, "pzyx,zk->pkyx", False)
    real_part = lax.all_to_all(part_re, "slab", split_axis=1, concat_axis=2, tiled=True)
    imag_part = lax.all_to_all(part_im, "slab", split_axis=1, concat_axis=2, tiled=True)
    real_part, imag_part = rotate(real_part, imag_part, cos_y, sin_y, "pzyx,yk->pzkx", False)
    factor = 1.0 / (columns * rows * depth)
    real_out = jnp.einsum(form_x, real_part, cos_x, precision=highest) - jnp.einsum(
        form_x, imag_part, sin_x, precision=highest
    )
    imag_out = jnp.einsum(form_x, imag_part, cos_x, precision=highest) + jnp.einsum(
        form_x, real_part, sin_x, precision=highest
    )
    stacked = jnp.stack([real_out * factor, imag_out * factor], axis=1)
    return stacked.reshape(count, planes, rows, columns)


def body(orbitals):
    count = orbitals.shape[0]
    grid_shape = orbitals.shape[1:]
    neighbour = shifted(orbitals, "band", 1)
    result = jnp.zeros_like(orbitals)
    for partners in (orbitals, neighbour):
        density = (orbitals[:, None] * partners[None, :]).reshape((count * count,) + grid_shape)
        field = potentials(density).reshape((count, count) + grid_shape)
        result = result - jnp.sum(field * partners[None], axis=1)
    return result


def solution(mesh):
    placed = (P("band", "slab", None, None),)
    return jax.shard_map(
        body, mesh=mesh, in_specs=placed, out_specs=P("band", "slab", None, None), check_vma=False
    )
```

profile of v0, /device:TPU:0, one launch (start us, length us, event | category | flops | bytes accessed | tf_op | source)
XLA Modules:
  0.0 544.5 jit_solution(10167117366901064484)
XLA Ops:
  0.0 2.7 broadcast_multiply_fusion.1
  18.6 7.3 %all-to-all-start.1 = ((f32[2,16,128,128]{3,1,0,2:T(8,128)}), f32[2,16,128,128]{3,1,0,2:T(8,128)}, u32[]{:S(2)}, u32[]{:S(2)}) async-start(f32[2,16,128,128]{3,1,0,2:T(8,128)} %copy.93), calls=%async_computation.1 | async-start | bytes 4194304 | tf_op jit(solution)/shard_map/all_to_all | solution.py:60
  25.9 3.7 fusion.140
  34.4 39.9 %all-to-all-done.1 = f32[2,16,128,128]{3,1,0,2:T(8,128)} async-done(((f32[2,16,128,128]{3,1,0,2:T(8,128)}), f32[2,16,128,128]{3,1,0,2:T(8,128)}, u32[]{:S(2)}, u32[]{:S(2)}) %all-to-all-start.1) | async-done | bytes 2097184 | tf_op jit(solution)/shard_map/all_to_all | solution.py:60
  74.3 4.6 all-to-all-start
  81.2 45.2 %all-to-all-done = f32[2,16,128,128]{3,1,0,2:T(8,128)} async-done(((f32[2,16,128,128]{3,1,0,2:T(8,128)}), f32[2,16,128,128]{3,1,0,2:T(8,128)}, u32[]{:S(2)}, u32[]{:S(2)}) %all-to-all-start) | async-done | bytes 2097184 | tf_op jit(solution)/shard_map/all_to_all | solution.py:59
  132.7 4.0 add_multiply_fusion.1
  141.4 2.7 add_bitcast_fusion.2
  146.7 4.3 all-to-all-start.2
  151.0 3.7 fusion.26
  159.6 39.2 %all-to-all-done.2 = f32[2,128,16,128]{3,2,0,1:T(8,128)} async-done(((f32[2,128,16,128]{3,2,0,1:T(8,128)}), f32[2,128,16,128]{3,2,0,1:T(8,128)}, u32[]{:S(2)}, u32[]{:S(2)}) %all-to-all-start.2) | async-done | bytes 2097184 | tf_op jit(solution)/shard_map/all_to_all | solution.py:74
  198.8 4.4 all-to-all-start.3
  203.5 3.2 copy.101
  206.7 44.3 %all-to-all-done.3 = f32[2,128,16,128]{3,2,0,1:T(8,128)} async-done(((f32[2,128,16,128]{3,2,0,1:T(8,128)}), f32[2,128,16,128]{3,2,0,1:T(8,128)}, u32[]{:S(2)}, u32[]{:S(2)}) %all-to-all-start.3) | async-done | bytes 2097184 | tf_op jit(solution)/shard_map/all_to_all | solution.py:75
  264.1 2.6 multiply_bitcast_fusion.3
  271.0 4.3 fusion
  288.6 2.6 copy.118
  291.2 4.3 all-to-all-start.5
  295.6 3.7 fusion.118
  304.1 39.3 %all-to-all-done.5 = f32[2,16,128,128]{3,1,0,2:T(8,128)} async-done(((f32[2,16,128,128]{3,1,0,2:T(8,128)}), f32[2,16,128,128]{3,1,0,2:T(8,128)}, u32[]{:S(2)}, u32[]{:S(2)}) %all-to-all-start.5) | async-done | bytes 2097184 | tf_op jit(solution)/shard_map/all_to_all | solution.py:60
  343.4 4.6 all-to-all-start.4
  349.8 45.7 %all-to-all-done.4 = f32[2,16,128,128]{3,1,0,2:T(8,128)} async-done(((f32[2,16,128,128]{3,1,0,2:T(8,128)}), f32[2,16,128,128]{3,1,0,2:T(8,128)}, u32[]{:S(2)}, u32[]{:S(2)}) %all-to-all-start.4) | async-done | bytes 2097184 | tf_op jit(solution)/shard_map/all_to_all | solution.py:59
  401.8 4.0 add_multiply_fusion
  410.5 2.7 add_bitcast_fusion
  413.2 2.6 copy.125
  415.8 4.3 all-to-all-start.6
  420.2 3.7 fusion.10
  428.8 39.2 %all-to-all-done.6 = f32[2,128,16,128]{3,2,0,1:T(8,128)} async-done(((f32[2,128,16,128]{3,2,0,1:T(8,128)}), f32[2,128,16,128]{3,2,0,1:T(8,128)}, u32[]{:S(2)}, u32[]{:S(2)}) %all-to-all-start.6) | async-done | bytes 2097184 | tf_op jit(solution)/shard_map/all_to_all | solution.py:74
  468.0 4.5 all-to-all-start.7
  474.4 45.8 %all-to-all-done.7 = f32[2,128,16,128]{3,2,0,1:T(8,128)} async-done(((f32[2,128,16,128]{3,2,0,1:T(8,128)}), f32[2,128,16,128]{3,2,0,1:T(8,128)}, u32[]{:S(2)}, u32[]{:S(2)}) %all-to-all-start.7) | async-done | bytes 2097184 | tf_op jit(solution)/shard_map/all_to_all | solution.py:75
  533.0 2.6 multiply_add_fusion
  539.8 2.8 fusion.1
  (78 shorter events, 114.9 us)
Async XLA Ops:
  13.6 2.4 copy-start.1
  18.6 55.7 %all-to-all-start.1 = ((f32[2,16,128,128]{3,1,0,2:T(8,128)}), f32[2,16,128,128]{3,1,0,2:T(8,128)}, u32[]{:S(2)}, u32[]{:S(2)}) async-start(f32[2,16,128,128]{3,1,0,2:T(8,128)} %copy.93), calls=%async_computation.1 | async-start | bytes 4194304 | tf_op jit(solution)/shard_map/all_to_all | solution.py:60
  74.3 52.2 %all-to-all-start = ((f32[2,16,128,128]{3,1,0,2:T(8,128)}), f32[2,16,128,128]{3,1,0,2:T(8,128)}, u32[]{:S(2)}, u32[]{:S(2)}) async-start(f32[2,16,128,128]{3,1,0,2:T(8,128)} %copy.88), calls=%async_computation | async-start | bytes 4194304 | tf_op jit(solution)/shard_map/all_to_all | solution.py:59
  81.2 49.3 %copy-start.5 = (f32[2,16,8,16,128]{4,1,2,3,0:T(8,128)}, f32[2,16,8,16,128]{4,1,2,3,0:T(8,128)S(1)}, u32[]{:S(2)}) copy-start(f32[2,16,8,16,128]{4,1,2,3,0:T(8,128)S(1)} %copy.94) | copy-start | bytes 6291460
  139.2 2.2 copy-start.4
  146.7 52.2 %all-to-all-start.2 = ((f32[2,128,16,128]{3,2,0,1:T(8,128)}), f32[2,128,16,128]{3,2,0,1:T(8,128)}, u32[]{:S(2)}, u32[]{:S(2)}) async-start(f32[2,128,16,128]{3,2,0,1:T(8,128)} %copy.100), calls=%async_computation.2 | async-start | bytes 4194304 | tf_op jit(solution)/shard_map/all_to_all | solution.py:74
  159.6 43.6 %copy-start = (f32[2,16,128,128]{3,2,1,0:T(8,128)S(1)}, f32[2,16,128,128]{3,2,1,0:T(8,128)}, u32[]{:S(2)}) copy-start(f32[2,16,128,128]{3,2,1,0:T(8,128)} %param.1) | copy-start | bytes 6291460
  198.8 52.2 %all-to-all-start.3 = ((f32[2,128,16,128]{3,2,0,1:T(8,128)}), f32[2,128,16,128]{3,2,0,1:T(8,128)}, u32[]{:S(2)}, u32[]{:S(2)}) async-start(f32[2,128,16,128]{3,2,0,1:T(8,128)} %copy.105), calls=%async_computation.3 | async-start | bytes 4194304 | tf_op jit(solution)/shard_map/all_to_all | solution.py:75
  203.2 67.8 %collective-permute-start = (f32[2,16,128,128]{3,2,1,0:T(8,128)S(1)}, f32[2,16,128,128]{3,2,1,0:T(8,128)}, u32[]{:S(2)}, u32[]{:S(2)}) collective-permute-start(f32[2,16,128,128]{3,2,1,0:T(8,128)S(1)} %copy-done), channel_id=1, source_target_pairs={{0,1},{1,2},{2,3},{3,0},{4,5},{5,6},{6,7},{7,4},{8,9},{9,10},{10,1... | collective-permute-start | bytes 6291464 | tf_op jit(solution)/shard_map/ppermute | solution.py:14
  252.8 2.2 copy-start.6
  286.4 2.2 copy-start.2
  291.2 52.2 %all-to-all-start.5 = ((f32[2,16,128,128]{3,1,0,2:T(8,128)}), f32[2,16,128,128]{3,1,0,2:T(8,128)}, u32[]{:S(2)}, u32[]{:S(2)}) async-start(f32[2,16,128,128]{3,1,0,2:T(8,128)} %copy.118), calls=%async_computation.5 | async-start | bytes 4194304 | tf_op jit(solution)/shard_map/all_to_all | solution.py:60
  343.4 52.2 %all-to-all-start.4 = ((f32[2,16,128,128]{3,1,0,2:T(8,128)}), f32[2,16,128,128]{3,1,0,2:T(8,128)}, u32[]{:S(2)}, u32[]{:S(2)}) async-start(f32[2,16,128,128]{3,1,0,2:T(8,128)} %copy.113), calls=%async_computation.4 | async-start | bytes 4194304 | tf_op jit(solution)/shard_map/all_to_all | solution.py:59
  349.8 49.8 %copy-start.7 = (f32[2,16,8,16,128]{4,1,2,3,0:T(8,128)}, f32[2,16,8,16,128]{4,1,2,3,0:T(8,128)S(1)}, u32[]{:S(2)}) copy-start(f32[2,16,8,16,128]{4,1,2,3,0:T(8,128)S(1)} %copy.119) | copy-start | bytes 6291460
  408.3 2.2 copy-start.3
  415.8 52.2 %all-to-all-start.6 = ((f32[2,128,16,128]{3,2,0,1:T(8,128)}), f32[2,128,16,128]{3,2,0,1:T(8,128)}, u32[]{:S(2)}, u32[]{:S(2)}) async-start(f32[2,128,16,128]{3,2,0,1:T(8,128)} %copy.125), calls=%async_computation.6 | async-start | bytes 4194304 | tf_op jit(solution)/shard_map/all_to_all | solution.py:74
  468.0 52.2 %all-to-all-start.7 = ((f32[2,128,16,128]{3,2,0,1:T(8,128)}), f32[2,128,16,128]{3,2,0,1:T(8,128)}, u32[]{:S(2)}, u32[]{:S(2)}) async-start(f32[2,128,16,128]{3,2,0,1:T(8,128)} %copy.130), calls=%async_computation.7 | async-start | bytes 4194304 | tf_op jit(solution)/shard_map/all_to_all | solution.py:75
  539.8 2.8 copy-start.8
where the time goes:
time: 554 us; the launch traced here: 544 us
  waiting for transfers between devices  338 us (61%)
  matrix products  117 us (21%)
  starting transfers between devices  38.6 us (7%)
  local copies, waits for them, and re-layouts  37.2 us (7%)
  other arithmetic  11.9 us (2%)
    all_to_all x2, waiting for transfers between devices, potentials(): lax.all_to_all(real_part, 'slab', split_axis=2, concat_axis=1, tiled=True)  90.9 us
    all_to_all x2, waiting for transfers between devices, potentials(): lax.all_to_all(part_im, 'slab', split_axis=1, concat_axis=2, tiled=True)  90.1 us
    all_to_all x2, waiting for transfers between devices, potentials(): lax.all_to_all(imag_part, 'slab', split_axis=2, concat_axis=1, tiled=True)  79.2 us
    all_to_all x2, waiting for transfers between devices, potentials(): lax.all_to_all(part_re, 'slab', split_axis=1, concat_axis=2, tiled=True)  78.3 us
    dot_general x8, matrix products, rotate(): real_cos = jnp.einsum(form, real_part, cosine, precision=highest)  21.7 us
    dot_general x8, matrix products, rotate(): imag_sin = jnp.einsum(form, imag_part, sine_table, precision=highest)  21.6 us
    dot_general x8, matrix products, rotate(): imag_cos = jnp.einsum(form, imag_part, cosine, precision=highest)  20.5 us
    dot_general x8, matrix products, rotate(): real_sin = jnp.einsum(form, real_part, sine_table, precision=highest)  18.9 us
  transfers between devices with their start and end apart: 9, of which 8 were waited for; matrix products, arithmetic and copies ran while one was open for 12% of the time, Pallas kernels for 0%

commit v1 on v0

--- a/solution.py
+++ b/solution.py
@@ -3,9 +3,21 @@
 import jax.numpy as jnp
 from jax import lax
 from jax.sharding import PartitionSpec as P
+from jax.lax import axis_index, ppermute, psum
 
 screen_width = 0.5
 highest = lax.Precision.HIGHEST
+
+
+def local_data_mix(base_x, dim_i, local_block):
+    plain, state_next = (base_x.shape[:dim_i], base_x.shape[dim_i + 1 :])
+    return jnp.moveaxis(base_x.reshape(*plain, local_block, -1, *state_next), dim_i, 0)
+
+
+def _spread_knots(own_rows, row_dim):
+    own_rows = jnp.moveaxis(own_rows, 0, row_dim)
+    t1 = own_rows.shape
+    return own_rows.reshape(*t1[:row_dim], t1[row_dim] * t1[row_dim + 1], *t1[row_dim + 2 :])
 
 
 def shifted(value, axis, steps):
@@ -57,7 +69,26 @@
     )
     real_part, imag_part = rotate(real_part, imag_part, cos_y, sin_y, "pzyx,yk->pzkx", True)
     part_re = lax.all_to_all(real_part, "slab", split_axis=2, concat_axis=1, tiled=True)
-    part_im = lax.all_to_all(imag_part, "slab", split_axis=2, concat_axis=1, tiled=True)
+
+    def cut_the_arrays(incoming_x, device_axis, field_in, block_here):
+        far_arr, formed = (psum(1, device_axis), axis_index(device_axis))
+        state_now = local_data_mix(incoming_x, field_in, far_arr)
+        stack_in = [state_now[formed]]
+        m = 1
+        while m < far_arr:
+            res = state_now[(formed + m) % far_arr]
+            stack_in.append(
+                ppermute(
+                    res,
+                    axis_name=device_axis,
+                    perm=[(ix, (ix + m) % far_arr) for ix in range(far_arr)],
+                )
+            )
+            m = m + 1
+        state_now = jnp.stack(stack_in)[(formed - jnp.arange(far_arr)) % far_arr]
+        return _spread_knots(state_now, block_here)
+
+    part_im = cut_the_arrays(imag_part, "slab", 2, 1)
     band_rows = part_re.shape[2]
     row_index = lax.axis_index("slab") * band_rows + jnp.arange(band_rows, dtype=jnp.int32)
     freq_z = frequency(jnp.arange(depth, dtype=jnp.int32), depth)

time: 554 us -> 560 us (1.011)
  waiting for transfers between devices: 338 us -> 282 us
  starting transfers between devices: 38.6 us -> 87.3 us
  local copies, waits for them, and re-layouts: 37.2 us -> 50.5 us
    ppermute x0 -> x14, waiting for transfers between devices: none -> 113 us  [cut_the_arrays(): ppermute(res, axis_name=device_axis, perm=[(ix, (ix + m) % far_arr) for i...]
    all_to_all x2, waiting for transfers between devices: 90.9 us -> 0.01 us  [potentials(): lax.all_to_all(real_part, 'slab', split_axis=2, concat_axis=1, tiled=True)]
    all_to_all x2 -> x0, waiting for transfers between devices: 79.2 us -> none  [potentials(): lax.all_to_all(imag_part, 'slab', split_axis=2, concat_axis=1, tiled=True)]
    ppermute x0 -> x14, starting transfers between devices: none -> 56.9 us  [cut_the_arrays(): ppermute(res, axis_name=device_axis, perm=[(ix, (ix + m) % far_arr) for i...]
    all_to_all x2 -> x0, starting transfers between devices: 11.7 us -> none  [potentials(): lax.all_to_all(imag_part, 'slab', split_axis=2, concat_axis=1, tiled=True)]
    unnamed x18 -> x36, local copies, waits for them, and re-layouts: 0.04 us -> 9.02 us
    gather x0 -> x2, local copies, waits for them, and re-layouts: none -> 5.71 us  [cut_the_arrays(): state_now = jnp.stack(stack_in)[(formed - jnp.arange(far_arr)) % far_arr]]
  transfers between devices with their start and end apart: 9 -> 21, of which waited for: 8 -> 10; matrix products, arithmetic and copies ran while one was open for 12% -> 13% of each run, Pallas kernels for 0% -> 0%
where the time goes in v1:
time: 560 us; the launch traced here: 551 us
  waiting for transfers between devices  282 us (50%)
  matrix products  118 us (21%)
  starting transfers between devices  87.3 us (16%)
  local copies, waits for them, and re-layouts  50.5 us (9%)
  other arithmetic  11.9 us (2%)
    ppermute x14, waiting for transfers between devices, cut_the_arrays(): ppermute(res, axis_name=device_axis, perm=[(ix, (ix + m) % far_arr) for i...  113 us
    all_to_all x2, waiting for transfers between devices, potentials(): lax.all_to_all(part_im, 'slab', split_axis=1, concat_axis=2, tiled=True)  90.1 us
    all_to_all x2, waiting for transfers between devices, potentials(): lax.all_to_all(part_re, 'slab', split_axis=1, concat_axis=2, tiled=True)  79.2 us
    ppermute x14, starting transfers between devices, cut_the_arrays(): ppermute(res, axis_name=device_axis, perm=[(ix, (ix + m) % far_arr) for i...  56.9 us
    dot_general x8, matrix products, rotate(): imag_sin = jnp.einsum(form, imag_part, sine_table, precision=highest)  25.1 us
    dot_general x8, matrix products, rotate(): imag_cos = jnp.einsum(form, imag_part, cosine, precision=highest)  21.9 us
    dot_general x8, matrix products, rotate(): real_sin = jnp.einsum(form, real_part, sine_table, precision=highest)  18.1 us
    dot_general x8, matrix products, rotate(): real_cos = jnp.einsum(form, real_part, cosine, precision=highest)  17.8 us
  transfers between devices with their start and end apart: 21, of which 10 were waited for; matrix products, arithmetic and copies ran while one was open for 13% of the time, Pallas kernels for 0%

profile of v1, /device:TPU:0, one launch (start us, length us, event | category | flops | bytes accessed | tf_op | source)
XLA Modules:
  0.0 550.7 jit_solution(18144979933912655045)
XLA Ops:
  18.6 7.3 %all-to-all-start = ((f32[2,16,128,128]{3,1,0,2:T(8,128)}), f32[2,16,128,128]{3,1,0,2:T(8,128)}, u32[]{:S(2)}, u32[]{:S(2)}) async-start(f32[2,16,128,128]{3,1,0,2:T(8,128)} %copy.130), calls=%async_computation | async-start | bytes 4194304 | tf_op jit(solution)/shard_map/all_to_all | solution.py:71
  31.6 4.7 collective-permute-start.6
  41.6 45.8 %collective-permute-done = f32[2,16,16,128]{3,2,1,0:T(8,128)} collective-permute-done((f32[2,16,16,128]{3,2,1,0:T(8,128)}, f32[2,16,16,128]{3,2,1,0:T(8,128)}, u32[]{:S(2)}, u32[]{:S(2)}) %collective-permute-start) | collective-permute-done | bytes 262176 | tf_op jit(solution)/shard_map/ppermute | solution.py:81
  87.5 9.3 %collective-permute-start.2 = (f32[2,16,16,128]{3,2,1,0:T(8,128)}, f32[2,16,16,128]{3,2,1,0:T(8,128)S(1)}, u32[]{:S(2)}, u32[]{:S(2)}) collective-permute-start(f32[2,16,16,128]{3,2,1,0:T(8,128)} %get-tuple-element.11), channel_id=1, source_target_pairs={{0,12},{4,16},{8,20},{12,24},{16,28},{20,0},{24,4},{28,8},{1,13},{... | collective-permute-start | bytes 786440 | tf_op jit(solution)/shard_map/ppermute | solution.py:81
  98.4 5.4 collective-permute-start.3
  105.4 9.9 %collective-permute-done.2 = f32[2,16,16,128]{3,2,1,0:T(8,128)S(1)} collective-permute-done((f32[2,16,16,128]{3,2,1,0:T(8,128)}, f32[2,16,16,128]{3,2,1,0:T(8,128)S(1)}, u32[]{:S(2)}, u32[]{:S(2)}) %collective-permute-start.2) | collective-permute-done | bytes 262176 | tf_op jit(solution)/shard_map/ppermute | solution.py:81
  116.1 3.0 collective-permute-done.3
  123.9 3.6 gather_fusion
  136.3 2.9 subtract_multiply_fusion.1
  139.2 5.2 add_multiply_fusion.1
  151.9 4.9 all-to-all-start.1
  156.8 3.7 fusion.26
  165.4 39.3 %all-to-all-done.1 = f32[2,128,16,128]{3,2,0,1:T(8,128)} async-done(((f32[2,128,16,128]{3,2,0,1:T(8,128)}), f32[2,128,16,128]{3,2,0,1:T(8,128)}, u32[]{:S(2)}, u32[]{:S(2)}) %all-to-all-start.1) | async-done | bytes 2097184 | tf_op jit(solution)/shard_map/all_to_all | solution.py:105
  204.8 4.4 all-to-all-start.2
  209.4 3.3 copy.144
  212.6 44.3 %all-to-all-done.2 = f32[2,128,16,128]{3,2,0,1:T(8,128)} async-done(((f32[2,128,16,128]{3,2,0,1:T(8,128)}), f32[2,128,16,128]{3,2,0,1:T(8,128)}, u32[]{:S(2)}, u32[]{:S(2)}) %all-to-all-start.2) | async-done | bytes 2097184 | tf_op jit(solution)/shard_map/all_to_all | solution.py:106
  277.0 4.3 fusion
  297.2 4.3 all-to-all-start.3
  309.6 3.3 collective-permute-start.14
  314.0 33.4 %collective-permute-done.8 = f32[2,16,16,128]{3,2,1,0:T(8,128)S(1)} collective-permute-done((f32[2,16,16,128]{3,2,1,0:T(8,128)S(1)}, f32[2,16,16,128]{3,2,1,0:T(8,128)S(1)}, u32[]{:S(2)}, u32[]{:S(2)}) %collective-permute-start.8) | collective-permute-done | bytes 262176 | tf_op jit(solution)/shard_map/ppermute | solution.py:81
  347.5 19.6 %collective-permute-start.10 = (f32[2,16,16,128]{3,2,1,0:T(8,128)S(1)}, f32[2,16,16,128]{3,2,1,0:T(8,128)S(1)}, u32[]{:S(2)}, u32[]{:S(2)}) collective-permute-start(f32[2,16,16,128]{3,2,1,0:T(8,128)S(1)} %get-tuple-element.18), channel_id=1, source_target_pairs={{0,12},{4,16},{8,20},{12,24},{16,28},{20,0},{24,4},{28,8},{1,13},{... | collective-permute-start | bytes 786440 | tf_op jit(solution)/shard_map/ppermute | solution.py:81
  367.1 6.0 %collective-permute-start.11 = (f32[2,16,16,128]{3,2,1,0:T(8,128)S(1)}, f32[2,16,16,128]{3,2,1,0:T(8,128)S(1)}, u32[]{:S(2)}, u32[]{:S(2)}) collective-permute-start(f32[2,16,16,128]{3,2,1,0:T(8,128)S(1)} %get-tuple-element.17), channel_id=1, source_target_pairs={{0,16},{4,20},{8,24},{12,28},{16,0},{20,4},{24,8},{28,12},{1,17},{... | collective-permute-start | bytes 786440 | tf_op jit(solution)/shard_map/ppermute | solution.py:81
  373.1 17.3 %collective-permute-done.10 = f32[2,16,16,128]{3,2,1,0:T(8,128)S(1)} collective-permute-done((f32[2,16,16,128]{3,2,1,0:T(8,128)S(1)}, f32[2,16,16,128]{3,2,1,0:T(8,128)S(1)}, u32[]{:S(2)}, u32[]{:S(2)}) %collective-permute-start.10) | collective-permute-done | bytes 262176 | tf_op jit(solution)/shard_map/ppermute | solution.py:81
  390.5 3.7 collective-permute-done.11
  405.2 2.9 subtract_multiply_fusion
  408.1 5.2 add_multiply_fusion
  420.9 4.8 all-to-all-start.4
  425.7 3.7 fusion.10
  434.4 39.9 %all-to-all-done.4 = f32[2,128,16,128]{3,2,0,1:T(8,128)} async-done(((f32[2,128,16,128]{3,2,0,1:T(8,128)}), f32[2,128,16,128]{3,2,0,1:T(8,128)}, u32[]{:S(2)}, u32[]{:S(2)}) %all-to-all-start.4) | async-done | bytes 2097184 | tf_op jit(solution)/shard_map/all_to_all | solution.py:105
  474.2 4.5 all-to-all-start.5
  480.6 45.8 %all-to-all-done.5 = f32[2,128,16,128]{3,2,0,1:T(8,128)} async-done(((f32[2,128,16,128]{3,2,0,1:T(8,128)}), f32[2,128,16,128]{3,2,0,1:T(8,128)}, u32[]{:S(2)}, u32[]{:S(2)}) %all-to-all-start.5) | async-done | bytes 2097184 | tf_op jit(solution)/shard_map/all_to_all | solution.py:106
  546.1 2.8 fusion.1
  (126 shorter events, 151.2 us)
Async XLA Ops:
  11.5 2.2 copy-start.1
  18.6 110.7 %all-to-all-start = ((f32[2,16,128,128]{3,1,0,2:T(8,128)}), f32[2,16,128,128]{3,1,0,2:T(8,128)}, u32[]{:S(2)}, u32[]{:S(2)}) async-start(f32[2,16,128,128]{3,1,0,2:T(8,128)} %copy.130), calls=%async_computation | async-start | bytes 4194304 | tf_op jit(solution)/shard_map/all_to_all | solution.py:71
  25.9 2.2 copy-start.2
  31.6 91.5 %collective-permute-start.6 = (f32[2,16,16,128]{3,2,1,0:T(8,128)}, f32[2,16,16,128]{3,2,1,0:T(8,128)S(1)}, u32[]{:S(2)}, u32[]{:S(2)}) collective-permute-start(f32[2,16,16,128]{3,2,1,0:T(8,128)} %get-tuple-element.7), channel_id=1, source_target_pairs={{0,28},{4,0},{8,4},{12,8},{16,12},{20,16},{24,20},{28,24},{1,29},{... | collective-permute-start | bytes 786440 | tf_op jit(solution)/shard_map/ppermute | solution.py:81
  36.3 85.1 %collective-permute-start.5 = (f32[2,16,16,128]{3,2,1,0:T(8,128)}, f32[2,16,16,128]{3,2,1,0:T(8,128)}, u32[]{:S(2)}, u32[]{:S(2)}) collective-permute-start(f32[2,16,16,128]{3,2,1,0:T(8,128)} %get-tuple-element.8), channel_id=1, source_target_pairs={{0,24},{4,28},{8,0},{12,4},{16,8},{20,12},{24,16},{28,20},{1,25},{... | collective-permute-start | bytes 786440 | tf_op jit(solution)/shard_map/ppermute | solution.py:81
  36.9 82.9 %collective-permute-start.4 = (f32[2,16,16,128]{3,2,1,0:T(8,128)}, f32[2,16,16,128]{3,2,1,0:T(8,128)}, u32[]{:S(2)}, u32[]{:S(2)}) collective-permute-start(f32[2,16,16,128]{3,2,1,0:T(8,128)} %get-tuple-element.9), channel_id=1, source_target_pairs={{0,20},{4,24},{8,28},{12,0},{16,4},{20,8},{24,12},{28,16},{1,21},{... | collective-permute-start | bytes 786440 | tf_op jit(solution)/shard_map/ppermute | solution.py:81
  36.9 61.5 %collective-permute-start.1 = (f32[2,16,16,128]{3,2,1,0:T(8,128)}, f32[2,16,16,128]{3,2,1,0:T(8,128)}, u32[]{:S(2)}, u32[]{:S(2)}) collective-permute-start(f32[2,16,16,128]{3,2,1,0:T(8,128)} %get-tuple-element.12), channel_id=1, source_target_pairs={{0,8},{4,12},{8,16},{12,20},{16,24},{20,28},{24,0},{28,4},{1,9},{5... | collective-permute-start | bytes 786440 | tf_op jit(solution)/shard_map/ppermute | solution.py:81
  38.4 49.1 %collective-permute-start = (f32[2,16,16,128]{3,2,1,0:T(8,128)}, f32[2,16,16,128]{3,2,1,0:T(8,128)}, u32[]{:S(2)}, u32[]{:S(2)}) collective-permute-start(f32[2,16,16,128]{3,2,1,0:T(8,128)} %get-tuple-element.13), channel_id=1, source_target_pairs={{0,4},{4,8},{8,12},{12,16},{16,20},{20,24},{24,28},{28,0},{1,5},{5... | collective-permute-start | bytes 786440 | tf_op jit(solution)/shard_map/ppermute | solution.py:81
  87.5 27.9 %collective-permute-start.2 = (f32[2,16,16,128]{3,2,1,0:T(8,128)}, f32[2,16,16,128]{3,2,1,0:T(8,128)S(1)}, u32[]{:S(2)}, u32[]{:S(2)}) collective-permute-start(f32[2,16,16,128]{3,2,1,0:T(8,128)} %get-tuple-element.11), channel_id=1, source_target_pairs={{0,12},{4,16},{8,20},{12,24},{16,28},{20,0},{24,4},{28,8},{1,13},{... | collective-permute-start | bytes 786440 | tf_op jit(solution)/shard_map/ppermute | solution.py:81
  98.4 20.6 %collective-permute-start.3 = (f32[2,16,16,128]{3,2,1,0:T(8,128)}, f32[2,16,16,128]{3,2,1,0:T(8,128)S(1)}, u32[]{:S(2)}, u32[]{:S(2)}) collective-permute-start(f32[2,16,16,128]{3,2,1,0:T(8,128)} %get-tuple-element.10), channel_id=1, source_target_pairs={{0,16},{4,20},{8,24},{12,28},{16,0},{20,4},{24,8},{28,12},{1,17},{... | collective-permute-start | bytes 786440 | tf_op jit(solution)/shard_map/ppermute | solution.py:81
  129.3 7.0 %copy-start.6 = (f32[2,8,16,16,128]{4,3,2,1,0:T(8,128)}, f32[2,8,16,16,128]{4,3,2,1,0:T(8,128)S(1)}, u32[]{:S(2)}) copy-start(f32[2,8,16,16,128]{4,3,2,1,0:T(8,128)S(1)} %copy.135) | copy-start | bytes 6291460
  139.2 5.2 copy-start.8
  151.9 52.8 %all-to-all-start.1 = ((f32[2,128,16,128]{3,2,0,1:T(8,128)}), f32[2,128,16,128]{3,2,0,1:T(8,128)}, u32[]{:S(2)}, u32[]{:S(2)}) async-start(f32[2,128,16,128]{3,2,0,1:T(8,128)} %copy.143), calls=%async_computation.1 | async-start | bytes 4194304 | tf_op jit(solution)/shard_map/all_to_all | solution.py:105
  165.4 43.7 %copy-start = (f32[2,16,128,128]{3,2,1,0:T(8,128)S(1)}, f32[2,16,128,128]{3,2,1,0:T(8,128)}, u32[]{:S(2)}) copy-start(f32[2,16,128,128]{3,2,1,0:T(8,128)} %param.1) | copy-start | bytes 6291460
  204.8 52.2 %all-to-all-start.2 = ((f32[2,128,16,128]{3,2,0,1:T(8,128)}), f32[2,128,16,128]{3,2,0,1:T(8,128)}, u32[]{:S(2)}, u32[]{:S(2)}) async-start(f32[2,128,16,128]{3,2,0,1:T(8,128)} %copy.148), calls=%async_computation.2 | async-start | bytes 4194304 | tf_op jit(solution)/shard_map/all_to_all | solution.py:106
  209.1 67.8 %collective-permute-start.7 = (f32[2,16,128,128]{3,2,1,0:T(8,128)S(1)}, f32[2,16,128,128]{3,2,1,0:T(8,128)}, u32[]{:S(2)}, u32[]{:S(2)}) collective-permute-start(f32[2,16,128,128]{3,2,1,0:T(8,128)S(1)} %copy-done), channel_id=1, source_target_pairs={{0,1},{1,2},{2,3},{3,0},{4,5},{5,6},{6,7},{7,4},{8,9},{9,10},{10,1... | collective-permute-start | bytes 6291464 | tf_op jit(solution)/shard_map/ppermute | solution.py:26
  258.8 2.2 copy-start.9
  290.2 2.2 copy-start.3
  297.2 101.0 %all-to-all-start.3 = ((f32[2,16,128,128]{3,1,0,2:T(8,128)}), f32[2,16,128,128]{3,1,0,2:T(8,128)}, u32[]{:S(2)}, u32[]{:S(2)}) async-start(f32[2,16,128,128]{3,1,0,2:T(8,128)} %copy.156), calls=%async_computation.3 | async-start | bytes 4194304 | tf_op jit(solution)/shard_map/all_to_all | solution.py:71
  301.5 2.2 copy-start.4
  306.2 41.3 %collective-permute-start.8 = (f32[2,16,16,128]{3,2,1,0:T(8,128)S(1)}, f32[2,16,16,128]{3,2,1,0:T(8,128)S(1)}, u32[]{:S(2)}, u32[]{:S(2)}) collective-permute-start(f32[2,16,16,128]{3,2,1,0:T(8,128)S(1)} %get-tuple-element.20), channel_id=1, source_target_pairs={{0,4},{4,8},{8,12},{12,16},{16,20},{20,24},{24,28},{28,0},{1,5},{5... | collective-permute-start | bytes 786440 | tf_op jit(solution)/shard_map/ppermute | solution.py:81
  308.1 59.0 %collective-permute-start.9 = (f32[2,16,16,128]{3,2,1,0:T(8,128)S(1)}, f32[2,16,16,128]{3,2,1,0:T(8,128)S(1)}, u32[]{:S(2)}, u32[]{:S(2)}) collective-permute-start(f32[2,16,16,128]{3,2,1,0:T(8,128)S(1)} %get-tuple-element.19), channel_id=1, source_target_pairs={{0,8},{4,12},{8,16},{12,20},{16,24},{20,28},{24,0},{28,4},{1,9},{5... | collective-permute-start | bytes 786440 | tf_op jit(solution)/shard_map/ppermute | solution.py:81
  309.6 84.7 %collective-permute-start.14 = (f32[2,16,16,128]{3,2,1,0:T(8,128)S(1)}, f32[2,16,16,128]{3,2,1,0:T(8,128)S(1)}, u32[]{:S(2)}, u32[]{:S(2)}) collective-permute-start(f32[2,16,16,128]{3,2,1,0:T(8,128)S(1)} %get-tuple-element.14), channel_id=1, source_target_pairs={{0,28},{4,0},{8,4},{12,8},{16,12},{20,16},{24,20},{28,24},{1,29},{... | collective-permute-start | bytes 786440 | tf_op jit(solution)/shard_map/ppermute | solution.py:81
  312.9 81.3 %collective-permute-start.13 = (f32[2,16,16,128]{3,2,1,0:T(8,128)S(1)}, f32[2,16,16,128]{3,2,1,0:T(8,128)S(1)}, u32[]{:S(2)}, u32[]{:S(2)}) collective-permute-start(f32[2,16,16,128]{3,2,1,0:T(8,128)S(1)} %get-tuple-element.15), channel_id=1, source_target_pairs={{0,24},{4,28},{8,0},{12,4},{16,8},{20,12},{24,16},{28,20},{1,25},{... | collective-permute-start | bytes 786440 | tf_op jit(solution)/shard_map/ppermute | solution.py:81
  313.0 81.2 %collective-permute-start.12 = (f32[2,16,16,128]{3,2,1,0:T(8,128)S(1)}, f32[2,16,16,128]{3,2,1,0:T(8,128)S(1)}, u32[]{:S(2)}, u32[]{:S(2)}) collective-permute-start(f32[2,16,16,128]{3,2,1,0:T(8,128)S(1)} %get-tuple-element.16), channel_id=1, source_target_pairs={{0,20},{4,24},{8,28},{12,0},{16,4},{20,8},{24,12},{28,16},{1,21},{... | collective-permute-start | bytes 786440 | tf_op jit(solution)/shard_map/ppermute | solution.py:81
  347.5 43.0 %collective-permute-start.10 = (f32[2,16,16,128]{3,2,1,0:T(8,128)S(1)}, f32[2,16,16,128]{3,2,1,0:T(8,128)S(1)}, u32[]{:S(2)}, u32[]{:S(2)}) collective-permute-start(f32[2,16,16,128]{3,2,1,0:T(8,128)S(1)} %get-tuple-element.18), channel_id=1, source_target_pairs={{0,12},{4,16},{8,20},{12,24},{16,28},{20,0},{24,4},{28,8},{1,13},{... | collective-permute-start | bytes 786440 | tf_op jit(solution)/shard_map/ppermute | solution.py:81
  367.1 27.0 %collective-permute-start.11 = (f32[2,16,16,128]{3,2,1,0:T(8,128)S(1)}, f32[2,16,16,128]{3,2,1,0:T(8,128)S(1)}, u32[]{:S(2)}, u32[]{:S(2)}) collective-permute-start(f32[2,16,16,128]{3,2,1,0:T(8,128)S(1)} %get-tuple-element.17), channel_id=1, source_target_pairs={{0,16},{4,20},{8,24},{12,28},{16,0},{20,4},{24,8},{28,12},{1,17},{... | collective-permute-start | bytes 786440 | tf_op jit(solution)/shard_map/ppermute | solution.py:81
  398.2 7.0 %copy-start.5 = (f32[2,8,16,16,128]{4,3,2,1,0:T(8,128)}, f32[2,8,16,16,128]{4,3,2,1,0:T(8,128)S(1)}, u32[]{:S(2)}) copy-start(f32[2,8,16,16,128]{4,3,2,1,0:T(8,128)S(1)} %copy.161) | copy-start | bytes 6291460
  408.1 5.2 copy-start.7
  420.9 53.4 %all-to-all-start.4 = ((f32[2,128,16,128]{3,2,0,1:T(8,128)}), f32[2,128,16,128]{3,2,0,1:T(8,128)}, u32[]{:S(2)}, u32[]{:S(2)}) async-start(f32[2,128,16,128]{3,2,0,1:T(8,128)} %copy.169), calls=%async_computation.4 | async-start | bytes 4194304 | tf_op jit(solution)/shard_map/all_to_all | solution.py:105
  474.2 52.2 %all-to-all-start.5 = ((f32[2,128,16,128]{3,2,0,1:T(8,128)}), f32[2,128,16,128]{3,2,0,1:T(8,128)}, u32[]{:S(2)}, u32[]{:S(2)}) async-start(f32[2,128,16,128]{3,2,0,1:T(8,128)} %copy.174), calls=%async_computation.5 | async-start | bytes 4194304 | tf_op jit(solution)/shard_map/all_to_all | solution.py:106
  546.0 2.8 copy-start.10
